TPU v7x, 32 devices: a whole 2x2x4 slice. The times are simulated.
32 devices in a mesh: dom: 2 (over y), grid: 4 (over z), band: 2 (over x), mem: 2 (over core).
Axes of the slice: x: 2, y: 2, z: 4, core: 2. Of those that a mesh axis runs over, the one named last changes fastest.
Arguments:
- grid_state: bfloat16 [4, 2048, 128], P(('dom', 'mem'), 'grid'), parts along dimension 0, may hold values from -6 to 6
- forcing: bfloat16 [4096, 128], P(('dom', 'grid')), parts along dimension 0, may hold values from -6 to 6
- boundary_mask: int32 [2048], P('grid'), may hold values 0 or 1
- edge_src: int32 [4, 4, 32], P('grid'), may hold values from 0 to 511
- edge_dst: int32 [4, 4, 32], P(None, 'grid'), may hold values from 0 to 127
- edge_count: int32 [4, 4], P(None, 'grid'), may hold values from 0 to 32, as said below
- edge_weight: float32 [4, 4, 32], P(None, 'grid'), may hold values from 0.1 to 1
- embed_weight: bfloat16 [128, 1024], P(None, 'band'), may hold values from -0.5 to 0.5
- attn_qkv: bfloat16 [1, 1024, 3, 1024], P(None, 'mem', None, 'band'), may hold values from -0.1875 to 0.1875
- attn_out: bfloat16 [1, 1024, 1024], P(None, 'band', 'mem'), may hold values from -0.1875 to 0.1875
- mlp_in: bfloat16 [1, 1024, 4096], P(None, 'mem', 'band'), may hold values from -0.1875 to 0.1875
- mlp_out: bfloat16 [1, 4096, 1024], P(None, 'band', 'mem'), may hold values from -0.09375 to 0.09375
- decode_weight: bfloat16 [1024, 128], P('band'), may hold values from -0.1875 to 0.1875
Outputs:
- next_state: bfloat16 [4, 2048, 128], P(('dom', 'mem'), 'grid'), parts along dimension 0
There are 2 independent parts, one for each index of `dom`. A program takes and returns all parts, laid end to end along the dimension named above; an argument that names none is the same for every part. Nothing has to cross between parts.
Inputs may be any that keep to these rules, and one draw needn't show every extreme that they name: Slots at or beyond edge_count[i, j] in a block are padding. In every draw some mesh band receives 32 live slots from every grid shard.
All inputs are finite; a program needn't handle non-finite values. No bound on the sum of `boundary_mask` on one device may be relied on, other than what follows from the above.
Results may differ from a plain program's by a relative error of at most 0.011.
Values may be sent and summed in bfloat16 or wider, within the bound.
No kernel may reach another device: no remote copies, remote signals or barrier semaphores. Data moves between devices by JAX's collectives and lax.ppermute only.
A program may use at most 64 MiB of HBM per device.

v0:
```python
import jax
import jax.numpy as jnp
from jax import lax
from jax.sharding import PartitionSpec as P

HEADS = 16
GP_DEV = 512
M_DEV = 128
WINDOW = 64


def extended(block, sides, width):
    for axis, dim in sides:
        count = lax.axis_size(axis)
        forward = [(i, i + 1) for i in range(count - 1)]
        backward = [(target, source) for source, target in forward]
        low = lax.ppermute(
            lax.slice_in_dim(block, block.shape[dim] - width, None, axis=dim), axis, forward
        )
        high = lax.ppermute(lax.slice_in_dim(block, 0, width, axis=dim), axis, backward)
        block = jnp.concatenate([low, block, high], axis=dim)
    return block


def rms_norm(values):
    return values * lax.rsqrt(jnp.mean(values * values, axis=-1, keepdims=True) + 1e-06)


def body(
    grid_state,
    forcing,
    boundary_mask,
    edge_src,
    edge_dst,
    edge_count,
    edge_weight,
    embed_weight,
    attn_qkv,
    attn_out,
    mlp_in,
    mlp_out,
    decode_weight,
):
    shards = lax.axis_size("grid")
    grid_index = lax.axis_index("grid")
    col_width = embed_weight.shape[1]
    grid_rows = grid_state[0]
    var_count = grid_rows.shape[1]
    slot_count = edge_dst.shape[2]
    sources = edge_src[0].reshape(-1)
    targets = edge_dst[:, 0].reshape(-1)
    live_slot = jnp.arange(slot_count, dtype=jnp.int32)[None, :] < edge_count[:, 0][:, None]
    weights = jnp.where(live_slot, edge_weight[:, 0], 0.0).reshape(-1)
    embedded = jax.nn.gelu(jnp.dot(grid_rows, embed_weight, preferred_element_type=jnp.float32))
    picked = embedded[sources].reshape(shards, slot_count, col_width)
    arrived = lax.all_to_all(
        picked.astype(jnp.bfloat16), "grid", split_axis=0, concat_axis=0, tiled=True
    ).astype(picked.dtype)
    latent = arrived.reshape(-1, col_width)
    mesh_part = jax.ops.segment_sum(latent * weights[:, None], targets, num_segments=M_DEV)
    mesh_in = lax.all_gather(mesh_part.astype(jnp.bfloat16), "band", axis=1, tiled=True)
    stream = mesh_in.astype(jnp.float32)
    mesh_rows = stream.shape[0]
    model_width = stream.shape[1]
    head_dim = model_width // HEADS
    local_heads = col_width // head_dim
    query_pos = grid_index * mesh_rows + jnp.arange(mesh_rows, dtype=jnp.int32)
    key_pos = grid_index * mesh_rows - WINDOW + jnp.arange(mesh_rows + 2 * WINDOW, dtype=jnp.int32)
    visible = (
        (jnp.abs(query_pos[:, None] - key_pos[None, :]) <= WINDOW)
        & (key_pos[None, :] >= 0)
        & (key_pos[None, :] < mesh_rows * shards)
    )
    w_qkv = lax.all_gather(attn_qkv[0], "mem", axis=0, tiled=True)
    w_out = lax.all_gather(attn_out[0], "mem", axis=1, tiled=True)
    w_in = lax.all_gather(mlp_in[0], "mem", axis=0, tiled=True)
    w_back = lax.all_gather(mlp_out[0], "mem", axis=1, tiled=True)
    normed = rms_norm(stream).astype(jnp.bfloat16)
    mixed_qkv = jnp.dot(
        normed, w_qkv.reshape(model_width, 3 * col_width), preferred_element_type=jnp.float32
    )
    mixed_qkv = mixed_qkv.reshape(mesh_rows, 3, local_heads, head_dim)
    queries = rms_norm(mixed_qkv[:, 0]).astype(jnp.bfloat16)
    keys_now = rms_norm(mixed_qkv[:, 1]).astype(jnp.bfloat16).reshape(mesh_rows, col_width)
    values = mixed_qkv[:, 2].astype(jnp.bfloat16).reshape(mesh_rows, col_width)
    padded = extended(jnp.stack([keys_now, values]), (("grid", 1),), WINDOW)
    near_keys = padded[0].reshape(-1, local_heads, head_dim)
    near_values = padded[1].reshape(-1, local_heads, head_dim)
    scores = jnp.einsum(
        "qhd,khd->hqk", queries, near_keys, preferred_element_type=jnp.float32
    ) * head_dim ** (-0.5)
    exp_scores = jnp.where(visible[None], jnp.exp(scores), 0.0)
    shares = (exp_scores / jnp.sum(exp_scores, axis=-1, keepdims=True)).astype(jnp.bfloat16)
    attended = jnp.einsum("hqk,khd->qhd", shares, near_values, preferred_element_type=jnp.float32)
    attended = attended.astype(jnp.bfloat16).reshape(mesh_rows, col_width)
    stream = stream + lax.psum(
        jnp.dot(attended, w_out, preferred_element_type=jnp.float32).astype(jnp.bfloat16), "band"
    ).astype(jnp.float32)
    normed = rms_norm(stream).astype(jnp.bfloat16)
    hidden = jax.nn.gelu(jnp.dot(normed, w_in, preferred_element_type=jnp.float32)).astype(
        jnp.bfloat16
    )
    stream = stream + lax.psum(
        jnp.dot(hidden, w_back, preferred_element_type=jnp.float32).astype(jnp.bfloat16), "band"
    ).astype(jnp.float32)
    mesh_out = stream.astype(jnp.bfloat16)
    mesh_cols = lax.dynamic_slice_in_dim(mesh_out, lax.axis_index("band") * col_width, col_width, 1)
    projected = lax.psum(
        jnp.dot(mesh_cols, decode_weight, preferred_element_type=jnp.float32).astype(jnp.bfloat16),
        "band",
    ).astype(jnp.float32)
    outgoing = (projected[targets] * weights[:, None]).reshape(shards, slot_count, var_count)
    returned = lax.all_to_all(
        outgoing.astype(jnp.bfloat16), "grid", split_axis=0, concat_axis=0, tiled=True
    ).astype(outgoing.dtype)
    decoded = jax.ops.segment_sum(returned.reshape(-1, var_count), sources, num_segments=GP_DEV)
    forced = boundary_mask[:, None] == 1
    result = jnp.where(forced, forcing.astype(jnp.float32), grid_rows.astype(jnp.float32) + decoded)
    return result.astype(jnp.bfloat16)[None]


def solution(mesh):
    return jax.shard_map(
        body,
        mesh=mesh,
        in_specs=(
            P(("dom", "mem"), "grid", None),
            P(("dom", "grid"), None),
            P("grid"),
            P("grid", None, None),
            P(None, "grid", None),
            P(None, "grid"),
            P(None, "grid", None),
            P(None, "band"),
            P(None, "mem", None, "band"),
            P(None, "band", "mem"),
            P(None, "mem", "band"),
            P(None, "band", "mem"),
            P("band", None),
        ),
        out_specs=P(("dom", "mem"), "grid", None),
        check_vma=False,
    )
```

profile of v0, /device:TPU:0, one launch (start us, length us, event | category | flops | bytes accessed | tf_op | source)
XLA Modules:
  0.0 162.2 jit_solution(17599511599854920596)
XLA Ops:
  6.6 2.7 %copy.14 = bf16[1,512,3,512]{1,3,2,0:T(8,128)(2,1)} copy(bf16[1,512,3,512]{3,1,2,0:T(8,128)(2,1)} %param.21) | data formatting | bytes 3145728 | tf_op args[8]
  10.0 1.5 gather_fusion
  11.5 6.3 %all-to-all-start = ((bf16[4,32,512]{2,1,0:T(8,128)(2,1)}), bf16[4,32,512]{2,1,0:T(8,128)(2,1)S(1)}, u32[]{:S(2)}, u32[]{:S(2)}) async-start(bf16[4,32,512]{2,1,0:T(8,128)(2,1)} %bitcast.2), calls=%async_computation | async-start | bytes 262144 | tf_op jit(solution)/shard_map/all_to_all | solution.py:56
  21.3 2.6 %all-to-all-done = bf16[4,32,512]{2,1,0:T(8,128)(2,1)S(1)} async-done(((bf16[4,32,512]{2,1,0:T(8,128)(2,1)}), bf16[4,32,512]{2,1,0:T(8,128)(2,1)S(1)}, u32[]{:S(2)}, u32[]{:S(2)}) %all-to-all-start) | async-done | bytes 131104 | tf_op jit(solution)/shard_map/all_to_all | solution.py:56
  23.9 1.5 scatter_custom_fusion
  25.4 5.6 %all_gather.15 = bf16[128,1024]{1,0:T(8,128)(2,1)S(1)} all-gather(bf16[128,512]{1,0:T(8,128)(2,1)S(1)} %convert_element_type.93), channel_id=1, replica_groups=mesh['dom'=2,'grid'=4,'band'=2,'mem'=2] {'band'}, dimensions={1}, use_global_device_ids=true | all-gather | bytes 393216 | tf_op jit(solution)/shard_map/all_gather | solution.py:61
  31.2 3.0 %fusion.39 = f32[128,3,8,64]{0,3,2,1:T(8,128)S(1)} fusion(bf16[3,8,64,1024]{3,2,1,0:T(8,128)(2,1)} %bitcast.72, bf16[128,1024]{1,0:T(8,128)(2,1)S(1)} %all_gather.15, f32[128]{0:T(128)S(1)} %add_rsqrt_fusion.3), kind=kOutput, calls=%fused_computation.48 | convolution fusion | flops 403046400 | bytes 4194816 | tf_op jit(solution)/shard_map/dot_general | solution.py:79
  34.5 3.0 %collective-permute-start = (bf16[2,64,512]{1,2,0:T(8,128)(2,1)S(1)}, bf16[2,64,512]{1,2,0:T(8,128)(2,1)S(1)}, u32[]{:S(2)}, u32[]{:S(2)}) collective-permute-start(bf16[2,64,512]{1,2,0:T(8,128)(2,1)S(1)} %get-tuple-element.11), channel_id=1, source_target_pairs={{0,4},{4,8},{8,12},{1,5},{5,9},{9,13},{2,6},{6,10},{10,14},{3,7},{... | collective-permute-start | bytes 393224 | tf_op jit(solution)/shard_map/ppermute | solution.py:17
  37.5 1.3 collective-permute-start.1
  38.8 2.5 %collective-permute-done = bf16[2,64,512]{1,2,0:T(8,128)(2,1)S(1)} collective-permute-done((bf16[2,64,512]{1,2,0:T(8,128)(2,1)S(1)}, bf16[2,64,512]{1,2,0:T(8,128)(2,1)S(1)}, u32[]{:S(2)}, u32[]{:S(2)}) %collective-permute-start) | collective-permute-done | bytes 131104 | tf_op jit(solution)/shard_map/ppermute | solution.py:17
  41.3 4.4 %collective-permute-done.1 = bf16[2,64,512]{1,2,0:T(8,128)(2,1)S(1)} collective-permute-done((bf16[2,64,512]{1,2,0:T(8,128)(2,1)S(1)}, bf16[2,64,512]{1,2,0:T(8,128)(2,1)S(1)}, u32[]{:S(2)}, u32[]{:S(2)}) %collective-permute-start.1) | collective-permute-done | bytes 131104 | tf_op jit(solution)/shard_map/ppermute | solution.py:20
  46.9 2.3 %convolution_convert_fusion = bf16[128,1024]{1,0:T(8,128)(2,1)} fusion(bf16[128,512]{0,1:T(8,128)(2,1)S(1)} %bitcast.80, bf16[1,512,1024]{2,1,0:T(8,128)(2,1)} %all-gather.11.cloned.1.call-done), kind=kOutput, calls=%fused_computation.13 | convolution fusion | flops 134348800 | bytes 1441792 | tf_op jit(solution)/shard_map/dot_general | solution.py:97
  50.6 20.6 %all-reduce.3.cloned.1.call-done = bf16[128,1024]{1,0:T(8,128)(2,1)} async-done(((bf16[128,1024]{1,0:T(8,128)(2,1)}), bf16[128,1024]{1,0:T(8,128)(2,1)}) %all-reduce.3.cloned.1.call-update) | async-done | bytes 262160 | tf_op jit(solution)/shard_map/psum | solution.py:96
  71.2 1.1 multiply_reduce_fusion
  72.4 13.9 %all-gather.13.cloned.1.call-done = bf16[1,1024,2048]{2,1,0:T(8,128)(2,1)} async-done(((bf16[1,512,2048]{2,1,0:T(8,128)(2,1)}), bf16[1,1024,2048]{2,1,0:T(8,128)(2,1)}) %all-gather.13.cloned.1.call-update) | async-done | bytes 4194320 | tf_op jit(solution)/shard_map/all_gather | solution.py:76
  86.3 16.3 %all-gather.15.cloned.1.call-done = bf16[1,2048,1024]{2,1,0:T(8,128)(2,1)} async-done(((bf16[1,2048,512]{2,1,0:T(8,128)(2,1)}), bf16[1,2048,1024]{2,1,0:T(8,128)(2,1)}) %all-gather.15.cloned.1.call-update) | async-done | bytes 4194320 | tf_op jit(solution)/shard_map/all_gather | solution.py:77
  102.6 5.9 %fusion.6 = bf16[128,1024]{1,0:T(8,128)(2,1)} fusion(bf16[1,2048,1024]{2,1,0:T(8,128)(2,1)} %all-gather.15.cloned.1.call-done, bf16[1,1024,2048]{2,1,0:T(8,128)(2,1)} %all-gather.13.cloned.1.call-done, f32[128]{0:T(128)S(1)} %add_rsqrt_fusion.2, bf16[128,1024]{1,0:T(8,128)(2,1)S(1)} %all_gather.15, bf16[128,1024]{1,0:T(8,128)(2,1)} %all-reduce.3.cloned.1.call-done), kind=kOutput, calls=%fused_computation.14 | convolution fusion | flops 1076887552 | bytes 9175552 | tf_op jit(solution)/shard_map/dot_general | solution.py:104
  108.5 24.5 %all-reduce.5.cloned.1.call-done = bf16[128,1024]{1,0:T(8,128)(2,1)} async-done(((bf16[128,1024]{1,0:T(8,128)(2,1)}), bf16[128,1024]{1,0:T(8,128)(2,1)}) %all-reduce.5.cloned.1.call-update) | async-done | bytes 262160 | tf_op jit(solution)/shard_map/psum | solution.py:103
  133.1 1.1 convolution_convert_fusion.2
  134.2 7.1 %psum.23 = bf16[128,128]{1,0:T(8,128)(2,1)S(1)} all-reduce(bf16[128,128]{1,0:T(8,128)(2,1)S(1)} %convolution_convert_fusion.2), channel_id=1, replica_groups=mesh['dom'=2,'grid'=4,'band'=2,'mem'=2] {'band'}, use_global_device_ids=true, to_apply=%region_8.9 | all-reduce | flops 16384 | bytes 65536 | tf_op jit(solution)/shard_map/psum | solution.py:108
  142.7 4.9 %all-to-all-start.1 = ((bf16[4,32,128]{2,1,0:T(8,128)(2,1)}), bf16[4,32,128]{2,1,0:T(8,128)(2,1)S(1)}, u32[]{:S(2)}, u32[]{:S(2)}) async-start(bf16[4,32,128]{2,1,0:T(8,128)(2,1)} %multiply_convert_fusion.5), calls=%async_computation.1 | async-start | bytes 65536 | tf_op jit(solution)/shard_map/all_to_all | solution.py:113
  147.6 5.6 %all-to-all-done.1 = bf16[4,32,128]{2,1,0:T(8,128)(2,1)S(1)} async-done(((bf16[4,32,128]{2,1,0:T(8,128)(2,1)}), bf16[4,32,128]{2,1,0:T(8,128)(2,1)S(1)}, u32[]{:S(2)}, u32[]{:S(2)}) %all-to-all-start.1) | async-done | bytes 32800 | tf_op jit(solution)/shard_map/all_to_all | solution.py:113
  153.2 1.4 scatter_custom_fusion.1
  154.6 0.8 fusion.47
  (74 shorter events, 8.5 us)
Async XLA Ops:
  6.5 2.9 %copy-start = (bf16[128,512]{1,0:T(8,128)(2,1)S(1)}, bf16[128,512]{1,0:T(8,128)(2,1)}, u32[]{:S(2)}) copy-start(bf16[128,512]{1,0:T(8,128)(2,1)} %param.20) | copy-start | bytes 393220
  6.5 2.8 %copy-start.4 = (s32[1,4,32]{2,1,0:T(4,128)S(1)}, s32[1,4,32]{2,1,0:T(4,128)}, u32[]{:S(2)}) copy-start(s32[1,4,32]{2,1,0:T(4,128)} %param.16) | copy-start | bytes 1540
  6.5 2.9 %copy-start.1 = (bf16[1,512,128]{2,1,0:T(8,128)(2,1)S(1)}, bf16[1,512,128]{2,1,0:T(8,128)(2,1)}, u32[]{:S(2)}) copy-start(bf16[1,512,128]{2,1,0:T(8,128)(2,1)} %param.13) | copy-start | bytes 393220
  6.5 12.1 %copy-start.8 = (s32[4,1]{0,1:T(1,128)S(1)}, s32[4,1]{0,1:T(1,128)}, u32[]{:S(2)}) copy-start(s32[4,1]{0,1:T(1,128)} %param.18) | copy-start | bytes 52
  6.5 12.8 %copy-start.6 = (f32[4,1,32]{2,1,0:T(1,128)S(1)}, f32[4,1,32]{2,1,0:T(1,128)}, u32[]{:S(2)}) copy-start(f32[4,1,32]{2,1,0:T(1,128)} %param.19) | copy-start | bytes 1540
  6.5 13.9 %copy-start.5 = (s32[4,1,32]{2,1,0:T(1,128)S(1)}, s32[4,1,32]{2,1,0:T(1,128)}, u32[]{:S(2)}) copy-start(s32[4,1,32]{2,1,0:T(1,128)} %param.17) | copy-start | bytes 1540
  6.6 24.6 %all-gather.9.cloned.1.call-start = ((), (), s32[]{:S(2)}) async-start(), calls=%async_computation.4 | async-start | bytes 4718592 | tf_op jit(solution)/shard_map/all_gather | solution.py:74
  11.5 12.4 %all-to-all-start = ((bf16[4,32,512]{2,1,0:T(8,128)(2,1)}), bf16[4,32,512]{2,1,0:T(8,128)(2,1)S(1)}, u32[]{:S(2)}, u32[]{:S(2)}) async-start(bf16[4,32,512]{2,1,0:T(8,128)(2,1)} %bitcast.2), calls=%async_computation | async-start | bytes 262144 | tf_op jit(solution)/shard_map/all_to_all | solution.py:56
  17.8 29.1 %all-gather.11.cloned.1.call-start = ((), (), s32[]{:S(2)}) async-start(), calls=%async_computation.5 | async-start | bytes 1572864 | tf_op jit(solution)/shard_map/all_gather | solution.py:75
  18.5 52.7 %all-reduce.3.cloned.1.call-start = ((), (), s32[]{:S(2)}) async-start(), calls=%async_computation.2 | async-start | bytes 524288 | tf_op jit(solution)/shard_map/psum | solution.py:96
  34.5 6.9 %collective-permute-start = (bf16[2,64,512]{1,2,0:T(8,128)(2,1)S(1)}, bf16[2,64,512]{1,2,0:T(8,128)(2,1)S(1)}, u32[]{:S(2)}, u32[]{:S(2)}) collective-permute-start(bf16[2,64,512]{1,2,0:T(8,128)(2,1)S(1)} %get-tuple-element.11), channel_id=1, source_target_pairs={{0,4},{4,8},{8,12},{1,5},{5,9},{9,13},{2,6},{6,10},{10,14},{3,7},{... | collective-permute-start | bytes 393224 | tf_op jit(solution)/shard_map/ppermute | solution.py:17
  37.5 8.3 %collective-permute-start.1 = (bf16[2,64,512]{1,2,0:T(8,128)(2,1)S(1)}, bf16[2,64,512]{1,2,0:T(8,128)(2,1)S(1)}, u32[]{:S(2)}, u32[]{:S(2)}) collective-permute-start(bf16[2,64,512]{1,2,0:T(8,128)(2,1)S(1)} %get-tuple-element.12), channel_id=1, source_target_pairs={{4,0},{8,4},{12,8},{5,1},{9,5},{13,9},{6,2},{10,6},{14,10},{7,3},{... | collective-permute-start | bytes 393224 | tf_op jit(solution)/shard_map/ppermute | solution.py:20
  49.2 37.1 %all-gather.13.cloned.1.call-start = ((), (), s32[]{:S(2)}) async-start(), calls=%async_computation.6 | async-start | bytes 6291456 | tf_op jit(solution)/shard_map/all_gather | solution.py:76
  49.8 52.8 %all-gather.15.cloned.1.call-start = ((), (), s32[]{:S(2)}) async-start(), calls=%async_computation.7 | async-start | bytes 6291456 | tf_op jit(solution)/shard_map/all_gather | solution.py:77
  50.4 82.7 %all-reduce.5.cloned.1.call-start = ((), (), s32[]{:S(2)}) async-start(), calls=%async_computation.3 | async-start | bytes 524288 | tf_op jit(solution)/shard_map/psum | solution.py:103
  72.3 60.7 %copy-start.2 = (bf16[512,128]{1,0:T(8,128)(2,1)S(1)}, bf16[512,128]{1,0:T(8,128)(2,1)}, u32[]{:S(2)}) copy-start(bf16[512,128]{1,0:T(8,128)(2,1)} %param.25) | copy-start | bytes 393220
  72.4 75.2 %copy-start.7 = (s32[512]{0:T(512)S(1)}, s32[512]{0:T(512)}, u32[]{:S(2)}) copy-start(s32[512]{0:T(512)} %param.15) | copy-start | bytes 6148
  72.4 82.2 %copy-start.3 = (bf16[512,128]{1,0:T(8,128)(2,1)S(1)}, bf16[512,128]{1,0:T(8,128)(2,1)}, u32[]{:S(2)}) copy-start(bf16[512,128]{1,0:T(8,128)(2,1)} %param.14) | copy-start | bytes 393220
  142.7 10.5 %all-to-all-start.1 = ((bf16[4,32,128]{2,1,0:T(8,128)(2,1)}), bf16[4,32,128]{2,1,0:T(8,128)(2,1)S(1)}, u32[]{:S(2)}, u32[]{:S(2)}) async-start(bf16[4,32,128]{2,1,0:T(8,128)(2,1)} %multiply_convert_fusion.5), calls=%async_computation.1 | async-start | bytes 65536 | tf_op jit(solution)/shard_map/all_to_all | solution.py:113
Sparse Core Ops, SparseCore 0:
  9.5 14.8 all-gather.8
  25.9 10.1 all-gather.10
  49.4 21.8 all-reduce.2
  72.6 13.6 all-gather.12
  87.7 14.8 all-gather.14
  108.6 24.4 all-reduce.4
where the time goes:
time: 163 us; the launch traced here: 162 us
  waiting for transfers between devices  92.3 us (57%)
  starting transfers between devices  15.7 us (10%)
  between operations  13.8 us (8%)
  matrix products  13.5 us (8%)
  blocking collectives  12.8 us (8%)
  other arithmetic  7.68 us (5%)
  local copies, waits for them, and re-layouts  6.48 us (4%)
    psum x1, waiting for transfers between devices, body(): lax.psum(jnp.dot(hidden, w_back, preferred_element_type=jnp.float32).asty...  24.5 us
    psum x1, waiting for transfers between devices, body(): lax.psum(jnp.dot(attended, w_out, preferred_element_type=jnp.float32).ast...  20.6 us
    all_gather x1, waiting for transfers between devices, body(): w_back = lax.all_gather(mlp_out[0], 'mem', axis=1, tiled=True)  16.3 us
    all_gather x1, waiting for transfers between devices, body(): w_in = lax.all_gather(mlp_in[0], 'mem', axis=0, tiled=True)  13.9 us
    psum x1, blocking collectives, body(): lax.psum(jnp.dot(mesh_cols, decode_weight, preferred_element_type=jnp.flo...  7.13 us
    all_to_all x1, starting transfers between devices, body(): lax.all_to_all(picked.astype(jnp.bfloat16), 'grid', split_axis=0, concat_...  6.34 us
    dot_general x1, matrix products, body(): jnp.dot(hidden, w_back, preferred_element_type=jnp.float32)  5.88 us
    all_gather x1, blocking collectives, body(): lax.all_gather(mesh_part.astype(jnp.bfloat16), 'band', axis=1, tiled=True)  5.64 us
  transfers between devices with their start and end apart: 10, of which 8 were waited for; matrix products, arithmetic and copies ran while one was open for 7% of the time, Pallas kernels for 0%

commit v1 on v0

--- a/solution.py
+++ b/solution.py
@@ -73,7 +73,9 @@
     )
     w_qkv = lax.all_gather(attn_qkv[0], "mem", axis=0, tiled=True)
     w_out = lax.all_gather(attn_out[0], "mem", axis=1, tiled=True)
-    w_in = lax.all_gather(mlp_in[0], "mem", axis=0, tiled=True)
+    w_in = jnp.concatenate(
+        lax.all_to_all(jnp.stack([mlp_in[0]] * lax.axis_size("mem")), "mem", 0, 0), axis=0
+    )
     w_back = lax.all_gather(mlp_out[0], "mem", axis=1, tiled=True)
     normed = rms_norm(stream).astype(jnp.bfloat16)
     mixed_qkv = jnp.dot(

time: 163 us -> 149 us (0.914)
  waiting for transfers between devices: 92.3 us -> 68 us
  starting transfers between devices: 15.7 us -> 21.2 us
  other arithmetic: 7.68 us -> 10.1 us
  matrix products: 13.5 us -> 15.3 us
    all_gather x1 -> x0, waiting for transfers between devices: 13.9 us -> none  [body(): w_in = lax.all_gather(mlp_in[0], 'mem', axis=0, tiled=True)]
    psum x1, waiting for transfers between devices: 20.6 us -> 13.4 us  [body(): lax.psum(jnp.dot(attended, w_out, preferred_element_type=jnp.float32).ast...]
    all_to_all x0 -> x1, starting transfers between devices: none -> 5.58 us  [body(): lax.all_to_all(jnp.stack([mlp_in[0]] * lax.axis_size('mem')), 'mem', 0, 0)]
    another operation x0 -> x1, other arithmetic: none -> 2.31 us  [body(): jnp.stack([mlp_in[0]] * lax.axis_size('mem'))]
    all_gather x1, waiting for transfers between devices: 16.3 us -> 14 us  [body(): w_back = lax.all_gather(mlp_out[0], 'mem', axis=1, tiled=True)]
    dot_general x1, matrix products: 0.38 us -> 2.14 us  [body(): jnp.einsum('hqk,khd->qhd', shares, near_values, preferred_element_type=jn...]
    unnamed x21 -> x25, local copies, waits for them, and re-layouts: 3.77 us -> 3.92 us
  transfers between devices with their start and end apart: 10 -> 10, of which waited for: 8 -> 7; matrix products, arithmetic and copies ran while one was open for 7% -> 12% of each run, Pallas kernels for 0% -> 0%
where the time goes in v1:
time: 149 us; the launch traced here: 148 us
  waiting for transfers between devices  68 us (46%)
  starting transfers between devices  21.2 us (14%)
  matrix products  15.3 us (10%)
  between operations  13.5 us (9%)
  blocking collectives  12.8 us (9%)
  other arithmetic  10.1 us (7%)
  local copies, waits for them, and re-layouts  7.32 us (5%)
    psum x1, waiting for transfers between devices, body(): lax.psum(jnp.dot(hidden, w_back, preferred_element_type=jnp.float32).asty...  24.6 us
    all_gather x1, waiting for transfers between devices, body(): w_back = lax.all_gather(mlp_out[0], 'mem', axis=1, tiled=True)  14 us
    psum x1, waiting for transfers between devices, body(): lax.psum(jnp.dot(attended, w_out, preferred_element_type=jnp.float32).ast...  13.4 us
    psum x1, blocking collectives, body(): lax.psum(jnp.dot(mesh_cols, decode_weight, preferred_element_type=jnp.flo...  7.13 us
    all_to_all x1, starting transfers between devices, body(): lax.all_to_all(picked.astype(jnp.bfloat16), 'grid', split_axis=0, concat_...  6.35 us
    dot_general x1, matrix products, body(): jnp.dot(hidden, w_back, preferred_element_type=jnp.float32)  5.91 us
    all_gather x1, blocking collectives, body(): lax.all_gather(mesh_part.astype(jnp.bfloat16), 'band', axis=1, tiled=True)  5.64 us
    all_to_all x1, starting transfers between devices, body(): lax.all_to_all(jnp.stack([mlp_in[0]] * lax.axis_size('mem')), 'mem', 0, 0)  5.58 us
  transfers between devices with their start and end apart: 10, of which 7 were waited for; matrix products, arithmetic and copies ran while one was open for 12% of the time, Pallas kernels for 0%

profile of v1, /device:TPU:0, one launch (start us, length us, event | category | flops | bytes accessed | tf_op | source)
XLA Modules:
  0.0 148.3 jit_solution(6553304721666789969)
XLA Ops:
  6.6 2.7 %copy.14 = bf16[1,512,3,512]{1,3,2,0:T(8,128)(2,1)} copy(bf16[1,512,3,512]{3,1,2,0:T(8,128)(2,1)} %param.21) | data formatting | bytes 3145728 | tf_op args[8]
  10.0 1.5 %gather_fusion = bf16[128,512]{1,0:T(8,128)(2,1)} fusion(bf16[512,512]{1,0:T(8,128)(2,1)S(1)} %fusion.13, s32[1024]{0:T(1024)S(1)} %pad_clamp_fusion.1), kind=kCustom, calls=%fused_computation | custom fusion | bytes 262656 | tf_op jit(solution)/shard_map/gather | solution.py:55
  11.5 6.4 %all-to-all-start = ((bf16[4,32,512]{2,1,0:T(8,128)(2,1)}), bf16[4,32,512]{2,1,0:T(8,128)(2,1)S(1)}, u32[]{:S(2)}, u32[]{:S(2)}) async-start(bf16[4,32,512]{2,1,0:T(8,128)(2,1)} %bitcast.2), calls=%async_computation | async-start | bytes 262144 | tf_op jit(solution)/shard_map/all_to_all | solution.py:56
  21.6 2.3 %all-to-all-done = bf16[4,32,512]{2,1,0:T(8,128)(2,1)S(1)} async-done(((bf16[4,32,512]{2,1,0:T(8,128)(2,1)}), bf16[4,32,512]{2,1,0:T(8,128)(2,1)S(1)}, u32[]{:S(2)}, u32[]{:S(2)}) %all-to-all-start) | async-done | bytes 131104 | tf_op jit(solution)/shard_map/all_to_all | solution.py:56
  23.9 1.5 scatter_custom_fusion
  25.4 5.6 %all_gather.12 = bf16[128,1024]{1,0:T(8,128)(2,1)S(1)} all-gather(bf16[128,512]{1,0:T(8,128)(2,1)S(1)} %convert_element_type.93), channel_id=1, replica_groups=mesh['dom'=2,'grid'=4,'band'=2,'mem'=2] {'band'}, dimensions={1}, use_global_device_ids=true | all-gather | bytes 393216 | tf_op jit(solution)/shard_map/all_gather | solution.py:61
  31.2 3.0 %fusion.33 = f32[128,3,8,64]{0,3,2,1:T(8,128)S(1)} fusion(bf16[3,8,64,1024]{3,2,1,0:T(8,128)(2,1)} %bitcast.65, bf16[128,1024]{1,0:T(8,128)(2,1)S(1)} %all_gather.12, f32[128]{0:T(128)S(1)} %add_rsqrt_fusion.3), kind=kOutput, calls=%fused_computation.48 | convolution fusion | flops 403046400 | bytes 4194816 | tf_op jit(solution)/shard_map/dot_general | solution.py:81
  34.5 3.0 %collective-permute-start = (bf16[2,64,512]{1,2,0:T(8,128)(2,1)S(1)}, bf16[2,64,512]{1,2,0:T(8,128)(2,1)S(1)}, u32[]{:S(2)}, u32[]{:S(2)}) collective-permute-start(bf16[2,64,512]{1,2,0:T(8,128)(2,1)S(1)} %get-tuple-element.11), channel_id=1, source_target_pairs={{0,4},{4,8},{8,12},{1,5},{5,9},{9,13},{2,6},{6,10},{10,14},{3,7},{... | collective-permute-start | bytes 393224 | tf_op jit(solution)/shard_map/ppermute | solution.py:17
  37.5 1.3 collective-permute-start.1
  38.8 2.5 %collective-permute-done = bf16[2,64,512]{1,2,0:T(8,128)(2,1)S(1)} collective-permute-done((bf16[2,64,512]{1,2,0:T(8,128)(2,1)S(1)}, bf16[2,64,512]{1,2,0:T(8,128)(2,1)S(1)}, u32[]{:S(2)}, u32[]{:S(2)}) %collective-permute-start) | collective-permute-done | bytes 131104 | tf_op jit(solution)/shard_map/ppermute | solution.py:17
  41.3 4.4 %collective-permute-done.1 = bf16[2,64,512]{1,2,0:T(8,128)(2,1)S(1)} collective-permute-done((bf16[2,64,512]{1,2,0:T(8,128)(2,1)S(1)}, bf16[2,64,512]{1,2,0:T(8,128)(2,1)S(1)}, u32[]{:S(2)}, u32[]{:S(2)}) %collective-permute-start.1) | collective-permute-done | bytes 131104 | tf_op jit(solution)/shard_map/ppermute | solution.py:20
  47.2 2.1 %convolution_convert_fusion.1 = bf16[8,64,128]{2,1,0:T(8,128)(2,1)} fusion(bf16[256,8,64]{0,2,1:T(8,128)(2,1)} %bitcast.70, f32[8,128,256]{2,1,0:T(8,128)S(1)} %fusion.3), kind=kOutput, calls=%fused_computation.14 | convolution fusion | flops 34145536 | bytes 1441792 | tf_op jit(solution)/shard_map/hqk,khd->qhd/dot_general | solution.py:96
  49.3 2.4 %convolution_convert_fusion = bf16[128,1024]{1,0:T(8,128)(2,1)} fusion(bf16[128,512]{0,1:T(8,128)(2,1)} %bitcast.73, bf16[1,512,1024]{2,1,0:T(8,128)(2,1)} %all-gather.9.cloned.1.call-done), kind=kOutput, calls=%fused_computation.12 | convolution fusion | flops 134348800 | bytes 1441792 | tf_op jit(solution)/shard_map/dot_general | solution.py:99
  52.3 2.3 %pad_maximum_fusion = bf16[2,512,2048]{2,1,0:T(8,128)(2,1)} fusion(bf16[1,512,2048]{2,1,0:T(8,128)(2,1)S(1)} %copy-done.1), kind=kLoop, calls=%fused_computation.4 | loop fusion | flops 2097152 | bytes 6291456 | tf_op jit(solution)/shard_map/stack | solution.py:77
  54.6 5.6 %all-to-all-start.1 = ((bf16[2,512,2048]{2,1,0:T(8,128)(2,1)}), bf16[2,512,2048]{2,1,0:T(8,128)(2,1)}, u32[]{:S(2)}, u32[]{:S(2)}) async-start(bf16[2,512,2048]{2,1,0:T(8,128)(2,1)} %pad_maximum_fusion), calls=%async_computation.1 | async-start | bytes 8388608 | tf_op jit(solution)/shard_map/all_to_all | solution.py:77
  60.4 13.4 %all-reduce.3.cloned.1.call-done = bf16[128,1024]{1,0:T(8,128)(2,1)} async-done(((bf16[128,1024]{1,0:T(8,128)(2,1)}), bf16[128,1024]{1,0:T(8,128)(2,1)}) %all-reduce.3.cloned.1.call-update) | async-done | bytes 262160 | tf_op jit(solution)/shard_map/psum | solution.py:98
  73.8 1.1 multiply_reduce_fusion
  74.9 14.0 %all-gather.11.cloned.1.call-done = bf16[1,2048,1024]{2,1,0:T(8,128)(2,1)} async-done(((bf16[1,2048,512]{2,1,0:T(8,128)(2,1)}), bf16[1,2048,1024]{2,1,0:T(8,128)(2,1)}) %all-gather.11.cloned.1.call-update) | async-done | bytes 4194320 | tf_op jit(solution)/shard_map/all_gather | solution.py:79
  88.9 5.9 %fusion.4 = bf16[128,1024]{1,0:T(8,128)(2,1)} fusion(bf16[1,2048,1024]{2,1,0:T(8,128)(2,1)} %all-gather.11.cloned.1.call-done, bf16[1024,2048]{1,0:T(8,128)(2,1)} %bitcast.19, f32[128]{0:T(128)S(1)} %add_rsqrt_fusion.2, bf16[128,1024]{1,0:T(8,128)(2,1)S(1)} %all_gather.12, bf16[128,1024]{1,0:T(8,128)(2,1)} %all-reduce.3.cloned.1.call-done), kind=kOutput, calls=%fused_computation.13 | convolution fusion | flops 1076887552 | bytes 9175552 | tf_op jit(solution)/shard_map/dot_general | solution.py:106
  94.9 24.6 %all-reduce.5.cloned.1.call-done = bf16[128,1024]{1,0:T(8,128)(2,1)} async-done(((bf16[128,1024]{1,0:T(8,128)(2,1)}), bf16[128,1024]{1,0:T(8,128)(2,1)}) %all-reduce.5.cloned.1.call-update) | async-done | bytes 262160 | tf_op jit(solution)/shard_map/psum | solution.py:105
  120.5 7.1 %psum.23 = bf16[128,128]{1,0:T(8,128)(2,1)S(1)} all-reduce(bf16[128,128]{1,0:T(8,128)(2,1)S(1)} %convolution_convert_fusion.2), channel_id=1, replica_groups=mesh['dom'=2,'grid'=4,'band'=2,'mem'=2] {'band'}, use_global_device_ids=true, to_apply=%region_8.9 | all-reduce | flops 16384 | bytes 65536 | tf_op jit(solution)/shard_map/psum | solution.py:110
  129.0 4.9 %all-to-all-start.2 = ((bf16[4,32,128]{2,1,0:T(8,128)(2,1)}), bf16[4,32,128]{2,1,0:T(8,128)(2,1)S(1)}, u32[]{:S(2)}, u32[]{:S(2)}) async-start(bf16[4,32,128]{2,1,0:T(8,128)(2,1)} %multiply_convert_fusion.8), calls=%async_computation.2 | async-start | bytes 65536 | tf_op jit(solution)/shard_map/all_to_all | solution.py:115
  134.0 5.6 %all-to-all-done.2 = bf16[4,32,128]{2,1,0:T(8,128)(2,1)S(1)} async-done(((bf16[4,32,128]{2,1,0:T(8,128)(2,1)}), bf16[4,32,128]{2,1,0:T(8,128)(2,1)S(1)}, u32[]{:S(2)}, u32[]{:S(2)}) %all-to-all-start.2) | async-done | bytes 32800 | tf_op jit(solution)/shard_map/all_to_all | solution.py:115
  139.6 1.4 scatter_custom_fusion.1
  (78 shorter events, 10.3 us)
Async XLA Ops:
  6.5 2.9 %copy-start = (bf16[128,512]{1,0:T(8,128)(2,1)S(1)}, bf16[128,512]{1,0:T(8,128)(2,1)}, u32[]{:S(2)}) copy-start(bf16[128,512]{1,0:T(8,128)(2,1)} %param.20) | copy-start | bytes 393220
  6.5 2.8 %copy-start.6 = (s32[1,4,32]{2,1,0:T(4,128)S(1)}, s32[1,4,32]{2,1,0:T(4,128)}, u32[]{:S(2)}) copy-start(s32[1,4,32]{2,1,0:T(4,128)} %param.16) | copy-start | bytes 1540
  6.5 2.9 %copy-start.2 = (bf16[1,512,128]{2,1,0:T(8,128)(2,1)S(1)}, bf16[1,512,128]{2,1,0:T(8,128)(2,1)}, u32[]{:S(2)}) copy-start(bf16[1,512,128]{2,1,0:T(8,128)(2,1)} %param.13) | copy-start | bytes 393220
  6.5 12.1 %copy-start.10 = (s32[4,1]{0,1:T(1,128)S(1)}, s32[4,1]{0,1:T(1,128)}, u32[]{:S(2)}) copy-start(s32[4,1]{0,1:T(1,128)} %param.18) | copy-start | bytes 52
  6.5 12.8 %copy-start.8 = (f32[4,1,32]{2,1,0:T(1,128)S(1)}, f32[4,1,32]{2,1,0:T(1,128)}, u32[]{:S(2)}) copy-start(f32[4,1,32]{2,1,0:T(1,128)} %param.19) | copy-start | bytes 1540
  6.5 14.2 %copy-start.7 = (s32[4,1,32]{2,1,0:T(1,128)S(1)}, s32[4,1,32]{2,1,0:T(1,128)}, u32[]{:S(2)}) copy-start(s32[4,1,32]{2,1,0:T(1,128)} %param.17) | copy-start | bytes 1540
  6.6 24.6 %all-gather.7.cloned.1.call-start = ((), (), s32[]{:S(2)}) async-start(), calls=%async_computation.5 | async-start | bytes 4718592 | tf_op jit(solution)/shard_map/all_gather | solution.py:74
  11.5 12.4 %all-to-all-start = ((bf16[4,32,512]{2,1,0:T(8,128)(2,1)}), bf16[4,32,512]{2,1,0:T(8,128)(2,1)S(1)}, u32[]{:S(2)}, u32[]{:S(2)}) async-start(bf16[4,32,512]{2,1,0:T(8,128)(2,1)} %bitcast.2), calls=%async_computation | async-start | bytes 262144 | tf_op jit(solution)/shard_map/all_to_all | solution.py:56
  17.8 31.5 %all-gather.9.cloned.1.call-start = ((), (), s32[]{:S(2)}) async-start(), calls=%async_computation.6 | async-start | bytes 1572864 | tf_op jit(solution)/shard_map/all_gather | solution.py:75
  18.5 55.2 %all-reduce.3.cloned.1.call-start = ((), (), s32[]{:S(2)}) async-start(), calls=%async_computation.3 | async-start | bytes 524288 | tf_op jit(solution)/shard_map/psum | solution.py:98
  34.5 6.8 %collective-permute-start = (bf16[2,64,512]{1,2,0:T(8,128)(2,1)S(1)}, bf16[2,64,512]{1,2,0:T(8,128)(2,1)S(1)}, u32[]{:S(2)}, u32[]{:S(2)}) collective-permute-start(bf16[2,64,512]{1,2,0:T(8,128)(2,1)S(1)} %get-tuple-element.11), channel_id=1, source_target_pairs={{0,4},{4,8},{8,12},{1,5},{5,9},{9,13},{2,6},{6,10},{10,14},{3,7},{... | collective-permute-start | bytes 393224 | tf_op jit(solution)/shard_map/ppermute | solution.py:17
  37.5 8.3 %collective-permute-start.1 = (bf16[2,64,512]{1,2,0:T(8,128)(2,1)S(1)}, bf16[2,64,512]{1,2,0:T(8,128)(2,1)S(1)}, u32[]{:S(2)}, u32[]{:S(2)}) collective-permute-start(bf16[2,64,512]{1,2,0:T(8,128)(2,1)S(1)} %get-tuple-element.12), channel_id=1, source_target_pairs={{4,0},{8,4},{12,8},{5,1},{9,5},{13,9},{6,2},{10,6},{14,10},{7,3},{... | collective-permute-start | bytes 393224 | tf_op jit(solution)/shard_map/ppermute | solution.py:20
  47.2 5.1 %copy-start.1 = (bf16[1,512,2048]{2,1,0:T(8,128)(2,1)S(1)}, bf16[1,512,2048]{2,1,0:T(8,128)(2,1)}, u32[]{:S(2)}) copy-start(bf16[1,512,2048]{2,1,0:T(8,128)(2,1)} %param.23) | copy-start | bytes 6291460
  51.7 37.2 %all-gather.11.cloned.1.call-start = ((), (), s32[]{:S(2)}) async-start(), calls=%async_computation.7 | async-start | bytes 6291456 | tf_op jit(solution)/shard_map/all_gather | solution.py:79
  54.6 20.3 %all-to-all-start.1 = ((bf16[2,512,2048]{2,1,0:T(8,128)(2,1)}), bf16[2,512,2048]{2,1,0:T(8,128)(2,1)}, u32[]{:S(2)}, u32[]{:S(2)}) async-start(bf16[2,512,2048]{2,1,0:T(8,128)(2,1)} %pad_maximum_fusion), calls=%async_computation.1 | async-start | bytes 8388608 | tf_op jit(solution)/shard_map/all_to_all | solution.py:77
  60.2 59.2 %all-reduce.5.cloned.1.call-start = ((), (), s32[]{:S(2)}) async-start(), calls=%async_computation.4 | async-start | bytes 524288 | tf_op jit(solution)/shard_map/psum | solution.py:105
  88.9 6.0 %copy-start.3 = (bf16[1,512,128]{2,1,0:T(8,128)(2,1)S(1)}, bf16[1,512,128]{2,1,0:T(8,128)(2,1)}, u32[]{:S(2)}) copy-start(bf16[1,512,128]{2,1,0:T(8,128)(2,1)} %param.13) | copy-start | bytes 393220
  88.9 30.6 %copy-start.4 = (bf16[512,128]{1,0:T(8,128)(2,1)S(1)}, bf16[512,128]{1,0:T(8,128)(2,1)}, u32[]{:S(2)}) copy-start(bf16[512,128]{1,0:T(8,128)(2,1)} %param.25) | copy-start | bytes 393220
  88.9 45.0 %copy-start.9 = (s32[512]{0:T(512)S(1)}, s32[512]{0:T(512)}, u32[]{:S(2)}) copy-start(s32[512]{0:T(512)} %param.15) | copy-start | bytes 6148
  88.9 52.0 %copy-start.5 = (bf16[512,128]{1,0:T(8,128)(2,1)S(1)}, bf16[512,128]{1,0:T(8,128)(2,1)}, u32[]{:S(2)}) copy-start(bf16[512,128]{1,0:T(8,128)(2,1)} %param.14) | copy-start | bytes 393220
  129.0 10.5 %all-to-all-start.2 = ((bf16[4,32,128]{2,1,0:T(8,128)(2,1)}), bf16[4,32,128]{2,1,0:T(8,128)(2,1)S(1)}, u32[]{:S(2)}, u32[]{:S(2)}) async-start(bf16[4,32,128]{2,1,0:T(8,128)(2,1)} %multiply_convert_fusion.8), calls=%async_computation.2 | async-start | bytes 65536 | tf_op jit(solution)/shard_map/all_to_all | solution.py:115
Sparse Core Ops, SparseCore 0:
  9.5 14.8 all-gather.6
  25.9 10.1 all-gather.8
  51.8 21.8 all-reduce.2
  75.2 13.6 all-gather.10
  94.9 24.4 all-reduce.4
